TPU v7x, 32 devices: a whole 2x2x4 slice. The times are simulated.
32 devices in a mesh: groups: 2 (over y), atoms: 8 (over z, x), samples: 2 (over core).
Axes of the slice: x: 2, y: 2, z: 4, core: 2. Of those that a mesh axis runs over, the one named last changes fastest.
Arguments:
- act: bfloat16 [16, 10240, 128], P('samples', ('groups', 'atoms')), parts along dimension 1, may hold values from -6 to 6
- grad_out: bfloat16 [16, 10240, 128], P('samples', ('groups', 'atoms')), parts along dimension 1, may hold values from -6 to 6
- pair: bfloat16 [320, 32, 16, 128], P(('groups', 'atoms')), parts along dimension 0, may hold values from -500 to 500
- w_query: bfloat16 [128, 128], replicated, may hold values from -0.5 to 0.5
- w_key: bfloat16 [128, 128], replicated, may hold values from -0.5 to 0.5
- w_value: bfloat16 [128, 128], replicated, may hold values from -0.5 to 0.5
- w_gate: bfloat16 [128, 128], replicated, may hold values from -0.5 to 0.5
- w_out: bfloat16 [128, 128], replicated, may hold values from -0.5 to 0.5
- w_pair: bfloat16 [16, 4], replicated, may hold values from -1.5 to 1.5
- w_token: float32 [4], replicated, may hold values from -2 to 2
- offsets: int32 [320], P(('groups', 'atoms')), parts along dimension 0, may hold values from -128 to 32, as said below
- atom_token: int32 [10240], P(('groups', 'atoms')), parts along dimension 0, may hold values from 0 to 639, never falling along the last dimension, each value on 1 to 24 neighbouring positions
- padding: int32 [16], P(('groups', 'atoms')), parts along dimension 0, may hold values from 0 to 64, as said below
Outputs:
- grad_act: bfloat16 [16, 10240, 128], P('samples', ('groups', 'atoms')), parts along dimension 1
- grad_pair: bfloat16 [320, 32, 16, 128], P(('groups', 'atoms'), 'samples'), parts along dimension 0
- grad_weights: float32 [10, 128, 128], P('groups'), parts along dimension 0
- grad_pair_weight: float32 [32, 4], P('groups'), parts along dimension 0
- grad_token_weight: float32 [8], P('groups'), parts along dimension 0
There are 2 independent parts, one for each index of `groups`. A program takes and returns all parts, laid end to end along the dimension named above; an argument that names none is the same for every part. Nothing has to cross between parts.
Inputs may be any that keep to these rules, and one draw needn't show every extreme that they name: Window w reads the 128 atoms that begin at 32 * w + offsets[w], moved into the complex. padding[r] atoms at the end of atom range r are padding. `atom_token`: the atoms of one token are contiguous, at most 24 of them.
All inputs are finite; a program needn't handle non-finite values.
Results may differ from a plain program's by a relative error of at most 0.025.
Values may be sent and summed in bfloat16 or wider, within the bound.
A program may use at most 128 MiB of HBM per device.

v0:
```python
import math
import jax
import jax.numpy as jnp
from jax import lax
from jax.sharding import PartitionSpec as P

MASKED = -1000000000.0


def with_halo(value, sides, width):
    for axis, dim in sides:
        count, length = (lax.axis_size(axis), value.shape[dim])
        up = [(i, (i + 1) % count) for i in range(count - 1)]
        down = [(j, i) for i, j in up]
        last = lax.slice_in_dim(value, length - width, length, axis=dim)
        initial = lax.slice_in_dim(value, 0, width, axis=dim)
        before = lax.ppermute(last, axis, up)
        after = lax.ppermute(initial, axis, down)
        value = jnp.concatenate([before, value, after], axis=dim)
    return value


def passed_along(value, axis, steps):
    count = lax.axis_size(axis)
    initial, last = (max(0, -steps), min(count, count - steps))
    return lax.ppermute(value, axis, [(source, source + steps) for source in range(initial, last)])


def attend(query, keys, values, gate_logit, grad_y, pair_bias, key_live):
    windows = keys.shape[0]
    head_count = pair_bias.shape[1]
    channels = query.shape[-1]
    head_dim = channels // head_count
    score_scale = 1.0 / math.sqrt(head_dim)
    query_heads = query.reshape(windows, -1, head_count, head_dim)
    key_heads = keys.reshape(windows, -1, head_count, head_dim)
    value_heads = values.reshape(windows, -1, head_count, head_dim)
    scores = (
        jnp.einsum("wihd,wjhd->whij", query_heads, key_heads, preferred_element_type=jnp.float32)
        * score_scale
        + pair_bias
    )
    scores = jnp.where(key_live[:, None, None, :], scores, MASKED)
    row_max = jnp.max(scores, axis=-1, keepdims=True)
    exponent = jnp.exp(scores - row_max)
    attn_probs = exponent / jnp.sum(exponent, axis=-1, keepdims=True)
    probs_b = attn_probs.astype(jnp.bfloat16)
    attended = jnp.einsum(
        "whij,wjhd->wihd", probs_b, value_heads, preferred_element_type=jnp.float32
    ).reshape(query.shape)
    gate_value = jax.nn.sigmoid(gate_logit)
    gated = (gate_value * attended).astype(jnp.bfloat16)
    d_attended = (grad_y * gate_value).astype(jnp.bfloat16)
    d_gate = (grad_y * attended * gate_value * (1.0 - gate_value)).astype(jnp.bfloat16)
    attended_heads = d_attended.reshape(windows, -1, head_count, head_dim)
    d_probs = jnp.einsum(
        "wihd,wjhd->whij", attended_heads, value_heads, preferred_element_type=jnp.float32
    )
    d_scores = attn_probs * (d_probs - jnp.sum(attn_probs * d_probs, axis=-1, keepdims=True))
    ds_b = d_scores.astype(jnp.bfloat16)
    d_query = (
        (
            jnp.einsum("whij,wjhd->wihd", ds_b, key_heads, preferred_element_type=jnp.float32)
            * score_scale
        )
        .astype(jnp.bfloat16)
        .reshape(query.shape)
    )
    d_keys = (
        jnp.einsum("whij,wihd->wjhd", ds_b, query_heads, preferred_element_type=jnp.float32)
        * score_scale
    )
    d_values = jnp.einsum(
        "whij,wihd->wjhd", probs_b, attended_heads, preferred_element_type=jnp.float32
    )
    return (gated, d_query, d_gate, d_keys, d_values, d_scores)


def per_device(
    act,
    grad_out,
    pair,
    w_query,
    w_key,
    w_value,
    w_gate,
    w_out,
    w_pair,
    w_token,
    offsets,
    atom_token,
    padding,
):
    sample_count, atom_count, channels = act.shape
    windows = offsets.shape[0]
    win_rows = atom_count // windows
    key_span = pair.shape[-1]
    ranges = lax.axis_size("atoms")
    anchor = lax.axis_index("atoms") * atom_count
    position = jnp.arange(atom_count, dtype=jnp.int32)
    is_live = position < atom_count - padding[0]
    atom_codes = jnp.where(is_live, atom_token + 1, 0)
    wide_codes = with_halo(atom_codes, (("atoms", 0),), key_span)
    starts = jnp.clip(
        anchor + win_rows * jnp.arange(windows, dtype=jnp.int32) + offsets,
        0,
        ranges * atom_count - key_span,
    )
    key_rows = starts[:, None] - anchor + key_span + jnp.arange(key_span, dtype=jnp.int32)[None, :]
    key_codes = wide_codes[key_rows]
    key_live = key_codes > 0
    same_token = key_codes[:, None, :] == (atom_token + 1).reshape(windows, win_rows)[:, :, None]
    pair_bias = jnp.einsum(
        "wicj,ch->whij", pair, w_pair, preferred_element_type=jnp.float32
    ) + w_token[None, :, None, None] * same_token[:, None, :, :].astype(jnp.float32)
    projection = jnp.concatenate([w_query, w_key, w_value, w_gate], axis=1)
    flat_act = act.reshape(sample_count * atom_count, channels)
    mixed = jnp.dot(flat_act, projection, preferred_element_type=jnp.float32).reshape(
        sample_count, atom_count, 4 * channels
    )
    query = mixed[..., :channels].astype(jnp.bfloat16)
    key_value = mixed[..., channels : 3 * channels].astype(jnp.bfloat16)
    gate_logit = mixed[..., 3 * channels :]
    wide_kv = with_halo(key_value, (("atoms", 1),), key_span)
    flat_grad = grad_out.reshape(sample_count * atom_count, channels)
    grad_y = jnp.dot(flat_grad, w_out.T, preferred_element_type=jnp.float32).reshape(
        sample_count, atom_count, channels
    )

    def one_sample(bias_sum, inputs):
        sample_query, sample_kv, sample_gate, sample_grad_y = inputs
        windowed = sample_kv[key_rows]
        gated, d_query, d_gate, d_keys, d_values, d_scores = attend(
            sample_query,
            windowed[..., :channels],
            windowed[..., channels:],
            sample_gate,
            sample_grad_y,
            pair_bias,
            key_live,
        )
        d_windowed = jnp.concatenate(
            [
                d_keys.reshape(windows, key_span, channels),
                d_values.reshape(windows, key_span, channels),
            ],
            axis=-1,
        )
        d_wide = jnp.zeros(sample_kv.shape, jnp.float32).at[key_rows].add(d_windowed)
        return (bias_sum + d_scores, (gated, d_query, d_gate, d_wide))

    bias_local, (gated, d_query, d_gate, d_wide) = lax.scan(
        one_sample, jnp.zeros(pair_bias.shape, jnp.float32), (query, wide_kv, gate_logit, grad_y)
    )
    inner_grad = d_wide[:, key_span : key_span + atom_count]
    from_upper = passed_along(d_wide[:, :key_span].astype(jnp.bfloat16), "atoms", -1).astype(
        jnp.float32
    )
    from_lower = passed_along(
        d_wide[:, key_span + atom_count :].astype(jnp.bfloat16), "atoms", 1
    ).astype(jnp.float32)
    kv_grad = (
        inner_grad.at[:, :key_span].add(from_lower).at[:, atom_count - key_span :].add(from_upper)
    )
    kv_rounded = kv_grad.astype(jnp.bfloat16)
    stacked = jnp.concatenate([d_query, kv_rounded, d_gate], axis=-1).reshape(
        sample_count * atom_count, 4 * channels
    )
    grad_act = (
        jnp.dot(stacked, projection.T, preferred_element_type=jnp.float32)
        .astype(jnp.bfloat16)
        .reshape(sample_count, atom_count, channels)
    )
    weight_part = jnp.dot(flat_act.T, stacked, preferred_element_type=jnp.float32)
    out_part = jnp.dot(gated.reshape(-1, channels).T, flat_grad, preferred_element_type=jnp.float32)
    pair_weight_part = jnp.einsum(
        "wicj,whij->ch", pair, bias_local, preferred_element_type=jnp.float32
    )
    token_part = jnp.sum(jnp.where(same_token[:, None, :, :], bias_local, 0.0), axis=(0, 2, 3))
    weight_sum, out_sum, grad_pair_weight, grad_token_weight = lax.psum(
        (weight_part, out_part, pair_weight_part, token_part), ("atoms", "samples")
    )
    grad_weights = jnp.concatenate(
        [weight_sum.reshape(channels, 4, channels).transpose(1, 0, 2), out_sum[None]], axis=0
    )
    sample_ways = lax.axis_size("samples")
    share_rows = win_rows // sample_ways
    bias_total = lax.psum(bias_local.astype(jnp.bfloat16), "samples").astype(jnp.float32)
    my_share = lax.dynamic_slice_in_dim(
        bias_total, lax.axis_index("samples") * share_rows, share_rows, 2
    )
    grad_pair = jnp.einsum(
        "whij,ch->wicj", my_share, w_pair.astype(jnp.float32), precision=lax.Precision.HIGHEST
    ).astype(jnp.bfloat16)
    return (grad_act, grad_pair, grad_weights, grad_pair_weight, grad_token_weight)


def solution(mesh):
    in_specs = (
        P("samples", ("groups", "atoms"), None),
        P("samples", ("groups", "atoms"), None),
        P(("groups", "atoms"), None, None, None),
        P(),
        P(),
        P(),
        P(),
        P(),
        P(),
        P(),
        P(("groups", "atoms")),
        P(("groups", "atoms")),
        P(("groups", "atoms")),
    )
    out_specs = (
        P("samples", ("groups", "atoms"), None),
        P(("groups", "atoms"), "samples", None, None),
        P("groups", None, None),
        P("groups", None),
        P("groups"),
    )
    return jax.shard_map(
        per_device, mesh=mesh, in_specs=in_specs, out_specs=out_specs, check_vma=False
    )
```

profile of v0, /device:TPU:8, one launch (start us, length us, event | category | flops | bytes accessed | tf_op | source)
XLA Modules:
  0.0 949.7 jit_solution(12060509717389246733)
XLA Ops:
  11.1 6.7 convolution_bitcast_fusion.1
  17.8 11.4 %copy.63 = f32[5120,512]{1,0:T(8,128)} copy(f32[5120,512]{0,1:T(8,128)} %convolution_bitcast_fusion.1) | data formatting | bytes 20971520 | tf_op jit(solution)/shard_map/reshape | solution.py:118
  29.2 4.7 convert.8
  45.0 4.2 collective-permute-start.1
  50.6 3.4 slice.115
  57.5 3.7 collective-permute-done
  63.1 9.4 gather_fusion.1
  78.5 686.5 %while.21 = (s32[]{:T(128)}, f32[20,4,32,128]{3,2,1,0:T(8,128)}, bf16[8,640,128]{2,1,0:T(8,128)(2,1)}, bf16[8,640,128]{1,2,0:T(8,128)(2,1)}, bf16[8,640,128]{1,2...) while((s32[]{:T(128)}, f32[20,4,32,128]{3,2,1,0:T(8,128)}, ...), condition=%wide.region_5.6_spmd.clone, body=%wide.region_0.5_spmd.clone.sunk | while | flops 135430016 | bytes 73126840 | solution.py:152
  79.6 8.1 gather_fusion
  99.7 7.5 convolution_bitcast_fusion.5
  116.8 7.5 fusion.113
  137.1 15.7 %scatter_custom_fusion.6 = f32[896,256]{1,0:T(8,128)} fusion(s32[2560]{0:T(1024)S(1)} %fusion.106, f32[2560,256]{1,0:T(8,128)} %bitcast.143, f32[]{:T(128)} %constant.105.clone.5..sunk), kind=kCustom, calls=%fused_computation.21.clone.1 | custom fusion | flops 655360 | bytes 918016 | tf_op jit(solution)/shard_map/while/body/eval_jaxpr/scatter-add | solution.py:149
  165.1 8.1 gather_fusion
  185.2 7.5 convolution_bitcast_fusion.5
  202.3 7.5 fusion.113
  213.1 3.4 fusion.110
  222.9 15.7 %scatter_custom_fusion.6 = f32[896,256]{1,0:T(8,128)} fusion(s32[2560]{0:T(1024)S(1)} %fusion.106, f32[2560,256]{1,0:T(8,128)} %bitcast.143, f32[]{:T(128)} %constant.105.clone.5..sunk), kind=kCustom, calls=%fused_computation.21.clone.1 | custom fusion | flops 655360 | bytes 918016 | tf_op jit(solution)/shard_map/while/body/eval_jaxpr/scatter-add | solution.py:149
  251.0 8.1 gather_fusion
  271.1 7.5 convolution_bitcast_fusion.5
  288.2 7.5 fusion.113
  308.8 15.7 %scatter_custom_fusion.6 = f32[896,256]{1,0:T(8,128)} fusion(s32[2560]{0:T(1024)S(1)} %fusion.106, f32[2560,256]{1,0:T(8,128)} %bitcast.143, f32[]{:T(128)} %constant.105.clone.5..sunk), kind=kCustom, calls=%fused_computation.21.clone.1 | custom fusion | flops 655360 | bytes 918016 | tf_op jit(solution)/shard_map/while/body/eval_jaxpr/scatter-add | solution.py:149
  336.8 8.1 gather_fusion
  356.9 7.5 convolution_bitcast_fusion.5
  374.0 7.5 fusion.113
  394.6 15.7 %scatter_custom_fusion.6 = f32[896,256]{1,0:T(8,128)} fusion(s32[2560]{0:T(1024)S(1)} %fusion.106, f32[2560,256]{1,0:T(8,128)} %bitcast.143, f32[]{:T(128)} %constant.105.clone.5..sunk), kind=kCustom, calls=%fused_computation.21.clone.1 | custom fusion | flops 655360 | bytes 918016 | tf_op jit(solution)/shard_map/while/body/eval_jaxpr/scatter-add | solution.py:149
  422.7 8.1 gather_fusion
  442.8 7.5 convolution_bitcast_fusion.5
  459.9 7.5 fusion.113
  480.5 15.7 %scatter_custom_fusion.6 = f32[896,256]{1,0:T(8,128)} fusion(s32[2560]{0:T(1024)S(1)} %fusion.106, f32[2560,256]{1,0:T(8,128)} %bitcast.143, f32[]{:T(128)} %constant.105.clone.5..sunk), kind=kCustom, calls=%fused_computation.21.clone.1 | custom fusion | flops 655360 | bytes 918016 | tf_op jit(solution)/shard_map/while/body/eval_jaxpr/scatter-add | solution.py:149
  508.5 8.1 gather_fusion
  528.6 7.5 convolution_bitcast_fusion.5
  545.7 7.5 fusion.113
  566.3 15.7 %scatter_custom_fusion.6 = f32[896,256]{1,0:T(8,128)} fusion(s32[2560]{0:T(1024)S(1)} %fusion.106, f32[2560,256]{1,0:T(8,128)} %bitcast.143, f32[]{:T(128)} %constant.105.clone.5..sunk), kind=kCustom, calls=%fused_computation.21.clone.1 | custom fusion | flops 655360 | bytes 918016 | tf_op jit(solution)/shard_map/while/body/eval_jaxpr/scatter-add | solution.py:149
  594.4 8.1 gather_fusion
  614.5 7.5 convolution_bitcast_fusion.5
  631.6 7.5 fusion.113
  652.2 15.7 %scatter_custom_fusion.6 = f32[896,256]{1,0:T(8,128)} fusion(s32[2560]{0:T(1024)S(1)} %fusion.106, f32[2560,256]{1,0:T(8,128)} %bitcast.143, f32[]{:T(128)} %constant.105.clone.5..sunk), kind=kCustom, calls=%fused_computation.21.clone.1 | custom fusion | flops 655360 | bytes 918016 | tf_op jit(solution)/shard_map/while/body/eval_jaxpr/scatter-add | solution.py:149
  680.3 8.1 gather_fusion
  700.4 7.5 convolution_bitcast_fusion.5
  717.5 7.5 fusion.113
  738.1 15.7 %scatter_custom_fusion.6 = f32[896,256]{1,0:T(8,128)} fusion(s32[2560]{0:T(1024)S(1)} %fusion.106, f32[2560,256]{1,0:T(8,128)} %bitcast.143, f32[]{:T(128)} %constant.105.clone.5..sunk), kind=kCustom, calls=%fused_computation.21.clone.1 | custom fusion | flops 655360 | bytes 918016 | tf_op jit(solution)/shard_map/while/body/eval_jaxpr/scatter-add | solution.py:149
  765.0 3.8 convert.9
  778.6 4.2 collective-permute-start.5
  784.5 30.8 %all-reduce = (f32[16,4]{0,1:T(4,128)}, f32[4]{0:T(128)}) all-reduce(f32[16,4]{0,1:T(4,128)S(1)} %fusion.22, f32[4]{0:T(128)S(1)} %select_reduce_fusion), channel_id=1, replica_groups=mesh['groups'=2,'atoms'=8,'samples'=2] {'atoms','samples'}, use_global_device_ids=true, to_apply=%region_9.10 | all-reduce | flops 68 | bytes 544 | tf_op jit(solution)/shard_map/psum | solution.py:180
  829.2 7.8 copy.54
  837.1 4.4 fusion.42
  842.3 5.1 convolution_convert_fusion
  850.1 91.1 %all-reduce.7.cloned.1.call-done = (f32[1,128,128]{2,1,0:T(8,128)}, f32[4,128,128]{2,1,0:T(8,128)}) async-done(((f32[1,128,128]{2,1,0:T(8,128)}, f32[4,128,128]{2,1,0:T(8,128)}), (f32[1,128,128]{2,1,0:T(8,128)}, f32[4,128,128]{2,1,0:T(8,128)})) %all-reduce.7.cloned.1.call-update) | async-done | bytes 327696 | tf_op jit(solution)/shard_map/psum | solution.py:180
  (422 shorter events, 429.2 us)
Async XLA Ops:
  7.2 65.5 %copy-start = (bf16[20,32,16,128]{3,2,1,0:T(8,128)(2,1)S(1)}, bf16[20,32,16,128]{3,2,1,0:T(8,128)(2,1)}, u32[]{:S(2)}) copy-start(bf16[20,32,16,128]{3,2,1,0:T(8,128)(2,1)} %param.21) | copy-start | bytes 7864324
  7.2 840.3 %all-reduce.5.cloned.1.call-start = ((), (), s32[]{:S(2)}) async-start(), calls=%async_computation | async-start | bytes 1310720 | tf_op jit(solution)/shard_map/psum | solution.py:188
  33.9 15.4 %copy-start.9 = (bf16[8,640,512]{2,1,0:T(8,128)(2,1)}, bf16[8,640,512]{2,1,0:T(8,128)(2,1)S(1)}, u32[]{:S(2)}) copy-start(bf16[8,640,512]{2,1,0:T(8,128)(2,1)S(1)} %convert.8) | copy-start | bytes 15728644
  33.9 8.6 copy-start.16
  35.1 39.5 %collective-permute-start.2 = (bf16[8,128,256]{2,1,0:T(8,128)(2,1)}, bf16[8,128,256]{2,1,0:T(8,128)(2,1)S(1)}, u32[]{:S(2)}, u32[]{:S(2)}) collective-permute-start(bf16[8,128,256]{2,1,0:T(8,128)(2,1)} %get-tuple-element.218), channel_id=1, source_target_pairs={{0,2},{2,4},{4,6},{6,8},{8,10},{10,12},{12,14},{1,3},{3,5},{5,7},{... | collective-permute-start | bytes 1572872 | tf_op jit(solution)/shard_map/ppermute | solution.py:17
  38.4 36.1 %collective-permute-start.3 = (bf16[8,128,256]{2,1,0:T(8,128)(2,1)}, bf16[8,128,256]{2,1,0:T(8,128)(2,1)}, u32[]{:S(2)}, u32[]{:S(2)}) collective-permute-start(bf16[8,128,256]{2,1,0:T(8,128)(2,1)} %get-tuple-element.219), channel_id=1, source_target_pairs={{2,0},{4,2},{6,4},{8,6},{10,8},{12,10},{14,12},{3,1},{5,3},{7,5},{... | collective-permute-start | bytes 1572872 | tf_op jit(solution)/shard_map/ppermute | solution.py:18
  42.5 18.7 %collective-permute-start = (s32[128]{0:T(128)S(1)}, s32[128]{0:T(128)S(1)}, u32[]{:S(2)}, u32[]{:S(2)}) collective-permute-start(s32[128]{0:T(128)S(1)} %get-tuple-element.226), channel_id=1, source_target_pairs={{0,2},{2,4},{4,6},{6,8},{8,10},{10,12},{12,14},{1,3},{3,5},{5,7},{... | collective-permute-start | bytes 1544 | tf_op jit(solution)/shard_map/ppermute | solution.py:17
  45.0 18.1 %collective-permute-start.1 = (s32[128]{0:T(128)S(1)}, s32[128]{0:T(128)S(1)}, u32[]{:S(2)}, u32[]{:S(2)}) collective-permute-start(s32[128]{0:T(128)S(1)} %get-tuple-element.227), channel_id=1, source_target_pairs={{2,0},{4,2},{6,4},{8,6},{10,8},{12,10},{14,12},{3,1},{5,3},{7,5},{... | collective-permute-start | bytes 1544 | tf_op jit(solution)/shard_map/ppermute | solution.py:18
  50.6 3.5 copy-start.19
  50.6 3.6 copy-start.15
  63.1 9.6 %copy-start.17 = (bf16[16,4]{0,1:T(4,128)(2,1)S(1)}, bf16[16,4]{0,1:T(4,128)(2,1)}, u32[]{:S(2)}) copy-start(bf16[16,4]{0,1:T(4,128)(2,1)} %param.27) | copy-start | bytes 388
  63.1 9.6 %copy-start.18 = (f32[4]{0:T(128)S(1)}, f32[4]{0:T(128)}, u32[]{:S(2)}) copy-start(f32[4]{0:T(128)} %param.28) | copy-start | bytes 52
  99.7 7.5 copy-start.10
  111.6 5.2 copy-start.5
  127.6 3.1 copy-start.2
  185.2 7.5 copy-start.10
  197.1 5.2 copy-start.5
  213.1 3.4 copy-start.2
  241.0 2.3 copy-start.3
  271.1 7.5 copy-start.10
  283.0 5.2 copy-start.5
  299.0 3.4 copy-start.2
  356.9 7.5 copy-start.10
  368.8 5.2 copy-start.5
  384.9 3.4 copy-start.2
  442.8 7.5 copy-start.10
  454.7 5.2 copy-start.5
  470.7 3.4 copy-start.2
  498.5 2.2 copy-start.3
  528.6 7.5 copy-start.10
  540.5 5.2 copy-start.5
  556.6 3.4 copy-start.2
  584.4 2.3 copy-start.3
  614.5 7.5 copy-start.10
  626.4 5.2 copy-start.5
  642.4 3.4 copy-start.2
  670.3 2.2 copy-start.3
  700.4 7.5 copy-start.10
  712.3 5.2 copy-start.5
  728.3 3.4 copy-start.2
  765.0 9.1 copy-start.8
  768.8 3.8 copy-start.6
  770.0 48.2 %collective-permute-start.4 = (bf16[8,128,256]{1,2,0:T(8,128)(2,1)}, bf16[8,128,256]{1,2,0:T(8,128)(2,1)S(1)}, u32[]{:S(2)}, u32[]{:S(2)}) collective-permute-start(bf16[8,128,256]{1,2,0:T(8,128)(2,1)} %get-tuple-element.221), channel_id=1, source_target_pairs={{0,2},{2,4},{4,6},{6,8},{8,10},{10,12},{12,14},{1,3},{3,5},{5,7},{... | collective-permute-start | bytes 1572872 | tf_op jit(solution)/shard_map/ppermute | solution.py:26
  778.6 42.0 %collective-permute-start.5 = (bf16[8,128,256]{1,2,0:T(8,128)(2,1)}, bf16[8,128,256]{1,2,0:T(8,128)(2,1)}, u32[]{:S(2)}, u32[]{:S(2)}) collective-permute-start(bf16[8,128,256]{1,2,0:T(8,128)(2,1)} %get-tuple-element.220), channel_id=1, source_target_pairs={{2,0},{4,2},{6,4},{8,6},{10,8},{12,10},{14,12},{3,1},{5,3},{7,5},{... | collective-permute-start | bytes 1572872 | tf_op jit(solution)/shard_map/ppermute | solution.py:26
  782.9 158.3 %all-reduce.7.cloned.1.call-start = ((), (), s32[]{:S(2)}) async-start(), calls=%async_computation.1 | async-start | bytes 655360 | tf_op jit(solution)/shard_map/psum | solution.py:180
  823.2 2.9 copy-start.11
  823.2 3.3 copy-start.12
  837.1 5.3 copy-start.14
  (30 other events, 52.2 us)
Sparse Core Ops, SparseCore 0:
  783.0 19.4 all-reduce.4
  847.6 93.5 all-reduce.6
where the time goes:
time: 956 us; the launch traced here: 950 us
  local copies, waits for them, and re-layouts  353 us (37%)
  other arithmetic  235 us (25%)
  matrix products  198 us (21%)
  waiting for transfers between devices  96.7 us (10%)
  blocking collectives  30.8 us (3%)
  starting transfers between devices  20.3 us (2%)
  between operations  15 us (2%)
    scatter-add x8, other arithmetic, one_sample(): jnp.zeros(sample_kv.shape, jnp.float32).at[key_rows].add(d_windowed)  125 us
    psum x1, waiting for transfers between devices, per_device(): lax.psum((weight_part, out_part, pair_weight_part, token_part), ('atoms',...  91.1 us
    dynamic_update_slice x48, local copies, waits for them, and re-layouts, per_device(): lax.scan(one_sample, jnp.zeros(pair_bias.shape, jnp.float32), (query, wid...  71.6 us
    gather x8, local copies, waits for them, and re-layouts, one_sample(): windowed = sample_kv[key_rows]  65.1 us
    dot_general x8, matrix products, attend(): jnp.einsum('whij,wjhd->wihd', probs_b, value_heads, preferred_element_typ...  60.3 us
    dot_general x8, matrix products, attend(): jnp.einsum('whij,wihd->wjhd', probs_b, attended_heads, preferred_element_...  59.8 us
    psum x1, blocking collectives, per_device(): lax.psum((weight_part, out_part, pair_weight_part, token_part), ('atoms',...  30.8 us
    while x128, local copies, waits for them, and re-layouts  28 us
  transfers between devices with their start and end apart: 8, of which 3 were waited for; matrix products, arithmetic and copies ran while one was open for 6% of the time, Pallas kernels for 0%

commit v1 on v0

--- a/solution.py
+++ b/solution.py
@@ -177,8 +177,14 @@
         "wicj,whij->ch", pair, bias_local, preferred_element_type=jnp.float32
     )
     token_part = jnp.sum(jnp.where(same_token[:, None, :, :], bias_local, 0.0), axis=(0, 2, 3))
-    weight_sum, out_sum, grad_pair_weight, grad_token_weight = lax.psum(
-        (weight_part, out_part, pair_weight_part, token_part), ("atoms", "samples")
+
+    def time_the_threads(incoming_x, ax_name, net_axis):
+        long_array = lax.psum(incoming_x, ax_name)
+        res = lax.psum(long_array, net_axis)
+        return res
+
+    weight_sum, out_sum, grad_pair_weight, grad_token_weight = time_the_threads(
+        (weight_part, out_part, pair_weight_part, token_part), "samples", "atoms"
     )
     grad_weights = jnp.concatenate(
         [weight_sum.reshape(channels, 4, channels).transpose(1, 0, 2), out_sum[None]], axis=0

time: 956 us -> 937 us (0.980)
  blocking collectives: 30.8 us -> 19.9 us
    psum x1 -> x2, waiting for transfers between devices: 91.1 us -> 67.9 us  [the longest x1 67.9 us: time_the_threads(): res = lax.psum(long_array, net_axis)]
    ppermute x2, waiting for transfers between devices: 0.01 us -> 19.4 us  [passed_along(): lax.ppermute(value, axis, [(source, source + steps) for source in range(i...]
    psum x1 -> x2, blocking collectives: 30.8 us -> 19.9 us  [the longest x1 17.4 us: time_the_threads(): res = lax.psum(long_array, net_axis)]
  transfers between devices with their start and end apart: 8 -> 9, of which waited for: 3 -> 5; matrix products, arithmetic and copies ran while one was open for 6% -> 5% of each run, Pallas kernels for 0% -> 0%
where the time goes in v1:
time: 937 us; the launch traced here: 929 us
  local copies, waits for them, and re-layouts  355 us (38%)
  other arithmetic  231 us (25%)
  matrix products  194 us (21%)
  waiting for transfers between devices  93 us (10%)
  starting transfers between devices  20.6 us (2%)
  blocking collectives  19.9 us (2%)
  between operations  14.8 us (2%)
    scatter-add x8, other arithmetic, one_sample(): jnp.zeros(sample_kv.shape, jnp.float32).at[key_rows].add(d_windowed)  125 us
    dynamic_update_slice x48, local copies, waits for them, and re-layouts, per_device(): lax.scan(one_sample, jnp.zeros(pair_bias.shape, jnp.float32), (query, wid...  71.6 us
    psum x1, waiting for transfers between devices, time_the_threads(): res = lax.psum(long_array, net_axis)  67.9 us
    gather x8, local copies, waits for them, and re-layouts, one_sample(): windowed = sample_kv[key_rows]  65.2 us
    dot_general x8, matrix products, attend(): jnp.einsum('whij,wjhd->wihd', probs_b, value_heads, preferred_element_typ...  60.5 us
    dot_general x8, matrix products, attend(): jnp.einsum('whij,wihd->wjhd', probs_b, attended_heads, preferred_element_...  60 us
    while x128, local copies, waits for them, and re-layouts  28 us
    convert_element_type x8, other arithmetic, attend(): ds_b = d_scores.astype(jnp.bfloat16)  27 us
  transfers between devices with their start and end apart: 9, of which 5 were waited for; matrix products, arithmetic and copies ran while one was open for 5% of the time, Pallas kernels for 0%

profile of v1, /device:TPU:8, one launch (start us, length us, event | category | flops | bytes accessed | tf_op | source)
XLA Modules:
  0.0 928.9 jit_solution(2196508342533310514)
XLA Ops:
  11.1 6.7 convolution_bitcast_fusion.1
  17.8 11.4 %copy.63 = f32[5120,512]{1,0:T(8,128)} copy(f32[5120,512]{0,1:T(8,128)} %convolution_bitcast_fusion.1) | data formatting | bytes 20971520 | tf_op jit(solution)/shard_map/reshape | solution.py:118
  29.2 4.7 convert.8
  45.0 4.2 collective-permute-start.1
  57.5 3.7 collective-permute-done
  63.1 9.4 %gather_fusion.1 = s32[2560]{0:T(1024)S(1)} fusion(s32[896]{0:T(1024)S(1)} %pad_add_fusion, s32[3072]{0:T(1024)S(1)} %pad_clamp_fusion.1), kind=kCustom, calls=%fused_computation.1 | custom fusion | bytes 30720 | tf_op jit(solution)/shard_map/gather | solution.py:110
  78.5 687.0 %while.21 = (s32[]{:T(128)}, f32[20,4,32,128]{3,2,1,0:T(8,128)}, bf16[8,640,128]{2,1,0:T(8,128)(2,1)}, bf16[8,640,128]{1,2,0:T(8,128)(2,1)}, bf16[8,640,128]{1,2...) while((s32[]{:T(128)}, f32[20,4,32,128]{3,2,1,0:T(8,128)}, ...), condition=%wide.region_5.6_spmd.clone, body=%wide.region_0.5_spmd.clone.sunk | while | flops 135430016 | bytes 73126840 | solution.py:152
  79.6 8.1 gather_fusion
  99.7 7.6 convolution_bitcast_fusion.6
  116.9 7.5 fusion.111
  137.1 15.7 %scatter_custom_fusion.6 = f32[896,256]{1,0:T(8,128)} fusion(s32[2560]{0:T(1024)S(1)} %fusion.104, f32[2560,256]{1,0:T(8,128)} %bitcast.142, f32[]{:T(128)} %constant.105.clone.5..sunk), kind=kCustom, calls=%fused_computation.21.clone.1 | custom fusion | flops 655360 | bytes 918016 | tf_op jit(solution)/shard_map/while/body/eval_jaxpr/scatter-add | solution.py:149
  165.2 8.1 gather_fusion
  185.3 7.6 convolution_bitcast_fusion.6
  202.4 7.5 fusion.111
  213.3 3.4 fusion.108
  223.0 15.7 %scatter_custom_fusion.6 = f32[896,256]{1,0:T(8,128)} fusion(s32[2560]{0:T(1024)S(1)} %fusion.104, f32[2560,256]{1,0:T(8,128)} %bitcast.142, f32[]{:T(128)} %constant.105.clone.5..sunk), kind=kCustom, calls=%fused_computation.21.clone.1 | custom fusion | flops 655360 | bytes 918016 | tf_op jit(solution)/shard_map/while/body/eval_jaxpr/scatter-add | solution.py:149
  251.1 8.1 gather_fusion
  271.2 7.6 convolution_bitcast_fusion.6
  288.4 7.5 fusion.111
  309.0 15.7 %scatter_custom_fusion.6 = f32[896,256]{1,0:T(8,128)} fusion(s32[2560]{0:T(1024)S(1)} %fusion.104, f32[2560,256]{1,0:T(8,128)} %bitcast.142, f32[]{:T(128)} %constant.105.clone.5..sunk), kind=kCustom, calls=%fused_computation.21.clone.1 | custom fusion | flops 655360 | bytes 918016 | tf_op jit(solution)/shard_map/while/body/eval_jaxpr/scatter-add | solution.py:149
  337.0 8.1 gather_fusion
  357.1 7.6 convolution_bitcast_fusion.6
  374.3 7.5 fusion.111
  394.9 15.7 %scatter_custom_fusion.6 = f32[896,256]{1,0:T(8,128)} fusion(s32[2560]{0:T(1024)S(1)} %fusion.104, f32[2560,256]{1,0:T(8,128)} %bitcast.142, f32[]{:T(128)} %constant.105.clone.5..sunk), kind=kCustom, calls=%fused_computation.21.clone.1 | custom fusion | flops 655360 | bytes 918016 | tf_op jit(solution)/shard_map/while/body/eval_jaxpr/scatter-add | solution.py:149
  422.9 8.1 gather_fusion
  443.0 7.6 convolution_bitcast_fusion.6
  460.2 7.5 fusion.111
  480.8 15.7 %scatter_custom_fusion.6 = f32[896,256]{1,0:T(8,128)} fusion(s32[2560]{0:T(1024)S(1)} %fusion.104, f32[2560,256]{1,0:T(8,128)} %bitcast.142, f32[]{:T(128)} %constant.105.clone.5..sunk), kind=kCustom, calls=%fused_computation.21.clone.1 | custom fusion | flops 655360 | bytes 918016 | tf_op jit(solution)/shard_map/while/body/eval_jaxpr/scatter-add | solution.py:149
  508.8 8.1 gather_fusion
  528.9 7.6 convolution_bitcast_fusion.6
  546.1 7.5 fusion.111
  566.7 15.7 %scatter_custom_fusion.6 = f32[896,256]{1,0:T(8,128)} fusion(s32[2560]{0:T(1024)S(1)} %fusion.104, f32[2560,256]{1,0:T(8,128)} %bitcast.142, f32[]{:T(128)} %constant.105.clone.5..sunk), kind=kCustom, calls=%fused_computation.21.clone.1 | custom fusion | flops 655360 | bytes 918016 | tf_op jit(solution)/shard_map/while/body/eval_jaxpr/scatter-add | solution.py:149
  594.7 8.1 gather_fusion
  614.9 7.6 convolution_bitcast_fusion.6
  632.0 7.5 fusion.111
  652.6 15.7 %scatter_custom_fusion.6 = f32[896,256]{1,0:T(8,128)} fusion(s32[2560]{0:T(1024)S(1)} %fusion.104, f32[2560,256]{1,0:T(8,128)} %bitcast.142, f32[]{:T(128)} %constant.105.clone.5..sunk), kind=kCustom, calls=%fused_computation.21.clone.1 | custom fusion | flops 655360 | bytes 918016 | tf_op jit(solution)/shard_map/while/body/eval_jaxpr/scatter-add | solution.py:149
  680.7 8.1 gather_fusion
  700.8 7.6 convolution_bitcast_fusion.6
  717.9 7.5 fusion.111
  738.6 15.7 %scatter_custom_fusion.6 = f32[896,256]{1,0:T(8,128)} fusion(s32[2560]{0:T(1024)S(1)} %fusion.104, f32[2560,256]{1,0:T(8,128)} %bitcast.142, f32[]{:T(128)} %constant.105.clone.5..sunk), kind=kCustom, calls=%fused_computation.21.clone.1 | custom fusion | flops 655360 | bytes 918016 | tf_op jit(solution)/shard_map/while/body/eval_jaxpr/scatter-add | solution.py:149
  765.4 3.8 convert.9
  772.6 4.3 collective-permute-start.5
  778.1 16.5 %collective-permute-done.4 = bf16[8,128,256]{1,2,0:T(8,128)(2,1)S(1)} collective-permute-done((bf16[8,128,256]{1,2,0:T(8,128)(2,1)S(1)}, bf16[8,128,256]{1,2,0:T(8,128)(2,1)S(1)}, u32[]{:S(2)}, u32[]{:S(2)}) %collective-permute-start.4) | collective-permute-done | bytes 524320 | tf_op jit(solution)/shard_map/ppermute | solution.py:26
  812.2 17.4 %all-reduce = (f32[16,4]{0,1:T(4,128)}, f32[4]{0:T(128)}) all-reduce(f32[16,4]{0,1:T(4,128)S(1)} %get-tuple-element.206, f32[4]{0:T(128)S(1)} %get-tuple-element.207), channel_id=1, replica_groups=mesh['groups'=2,'atoms'=8,'samples'=2] {'atoms'}, use_global_device_ids=true, to_apply=%region_12.13 | all-reduce | flops 68 | bytes 544 | tf_op jit(solution)/shard_map/psum | solution.py:183
  829.7 5.6 pad_maximum_fusion.1
  835.3 7.9 copy.54
  845.0 5.1 convolution_convert_fusion
  852.7 67.9 %all-reduce.10.cloned.1.call-done = (f32[1,128,128]{2,1,0:T(8,128)}, f32[4,128,128]{2,1,0:T(8,128)}) async-done(((f32[1,128,128]{2,1,0:T(8,128)}, f32[4,128,128]{2,1,0:T(8,128)}), (f32[1,128,128]{2,1,0:T(8,128)}, f32[4,128,128]{2,1,0:T(8,128)})) %all-reduce.10.cloned.1.call-update) | async-done | bytes 327696 | tf_op jit(solution)/shard_map/psum | solution.py:183
  (434 shorter events, 430.4 us)
Async XLA Ops:
  7.2 65.5 %copy-start = (bf16[20,32,16,128]{3,2,1,0:T(8,128)(2,1)S(1)}, bf16[20,32,16,128]{3,2,1,0:T(8,128)(2,1)}, u32[]{:S(2)}) copy-start(bf16[20,32,16,128]{3,2,1,0:T(8,128)(2,1)} %param.21) | copy-start | bytes 7864324
  7.2 836.0 %all-reduce.12.cloned.1.call-start = ((), (), s32[]{:S(2)}) async-start(), calls=%async_computation.2 | async-start | bytes 655360 | tf_op jit(solution)/shard_map/psum | solution.py:182
  33.9 15.4 %copy-start.9 = (bf16[8,640,512]{2,1,0:T(8,128)(2,1)}, bf16[8,640,512]{2,1,0:T(8,128)(2,1)S(1)}, u32[]{:S(2)}) copy-start(bf16[8,640,512]{2,1,0:T(8,128)(2,1)S(1)} %convert.8) | copy-start | bytes 15728644
  33.9 8.6 copy-start.20
  35.1 39.5 %collective-permute-start.2 = (bf16[8,128,256]{2,1,0:T(8,128)(2,1)}, bf16[8,128,256]{2,1,0:T(8,128)(2,1)S(1)}, u32[]{:S(2)}, u32[]{:S(2)}) collective-permute-start(bf16[8,128,256]{2,1,0:T(8,128)(2,1)} %get-tuple-element.222), channel_id=1, source_target_pairs={{0,2},{2,4},{4,6},{6,8},{8,10},{10,12},{12,14},{1,3},{3,5},{5,7},{... | collective-permute-start | bytes 1572872 | tf_op jit(solution)/shard_map/ppermute | solution.py:17
  38.5 36.1 %collective-permute-start.3 = (bf16[8,128,256]{2,1,0:T(8,128)(2,1)}, bf16[8,128,256]{2,1,0:T(8,128)(2,1)}, u32[]{:S(2)}, u32[]{:S(2)}) collective-permute-start(bf16[8,128,256]{2,1,0:T(8,128)(2,1)} %get-tuple-element.223), channel_id=1, source_target_pairs={{2,0},{4,2},{6,4},{8,6},{10,8},{12,10},{14,12},{3,1},{5,3},{7,5},{... | collective-permute-start | bytes 1572872 | tf_op jit(solution)/shard_map/ppermute | solution.py:18
  42.5 18.7 %collective-permute-start = (s32[128]{0:T(128)S(1)}, s32[128]{0:T(128)S(1)}, u32[]{:S(2)}, u32[]{:S(2)}) collective-permute-start(s32[128]{0:T(128)S(1)} %get-tuple-element.230), channel_id=1, source_target_pairs={{0,2},{2,4},{4,6},{6,8},{8,10},{10,12},{12,14},{1,3},{3,5},{5,7},{... | collective-permute-start | bytes 1544 | tf_op jit(solution)/shard_map/ppermute | solution.py:17
  45.0 18.1 %collective-permute-start.1 = (s32[128]{0:T(128)S(1)}, s32[128]{0:T(128)S(1)}, u32[]{:S(2)}, u32[]{:S(2)}) collective-permute-start(s32[128]{0:T(128)S(1)} %get-tuple-element.231), channel_id=1, source_target_pairs={{2,0},{4,2},{6,4},{8,6},{10,8},{12,10},{14,12},{3,1},{5,3},{7,5},{... | collective-permute-start | bytes 1544 | tf_op jit(solution)/shard_map/ppermute | solution.py:18
  63.1 9.6 %copy-start.21 = (bf16[16,4]{0,1:T(4,128)(2,1)S(1)}, bf16[16,4]{0,1:T(4,128)(2,1)}, u32[]{:S(2)}) copy-start(bf16[16,4]{0,1:T(4,128)(2,1)} %param.27) | copy-start | bytes 388
  63.1 9.6 %copy-start.22 = (f32[4]{0:T(128)S(1)}, f32[4]{0:T(128)}, u32[]{:S(2)}) copy-start(f32[4]{0:T(128)} %param.28) | copy-start | bytes 52
  99.7 7.6 copy-start.10
  111.6 5.2 copy-start.5
  127.7 3.1 copy-start.2
  155.2 2.2 copy-start.3
  185.3 7.6 copy-start.10
  197.2 5.2 copy-start.5
  213.3 3.4 copy-start.2
  241.1 2.3 copy-start.3
  271.2 7.6 copy-start.10
  283.1 5.2 copy-start.5
  299.2 3.4 copy-start.2
  357.1 7.6 copy-start.10
  369.0 5.2 copy-start.5
  385.1 3.4 copy-start.2
  443.0 7.6 copy-start.10
  454.9 5.2 copy-start.5
  471.0 3.4 copy-start.2
  528.9 7.6 copy-start.10
  540.8 5.2 copy-start.5
  556.9 3.4 copy-start.2
  584.7 2.2 copy-start.3
  614.8 7.6 copy-start.10
  626.8 5.2 copy-start.5
  642.8 3.4 copy-start.2
  670.7 2.3 copy-start.3
  700.8 7.6 copy-start.10
  712.7 5.2 copy-start.5
  728.8 3.4 copy-start.2
  765.4 6.8 copy-start.8
  769.5 7.4 copy-start.12
  769.5 7.4 copy-start.16
  769.5 25.0 %collective-permute-start.4 = (bf16[8,128,256]{1,2,0:T(8,128)(2,1)S(1)}, bf16[8,128,256]{1,2,0:T(8,128)(2,1)S(1)}, u32[]{:S(2)}, u32[]{:S(2)}) collective-permute-start(bf16[8,128,256]{1,2,0:T(8,128)(2,1)S(1)} %get-tuple-element.225), channel_id=1, source_target_pairs={{0,2},{2,4},{4,6},{6,8},{8,10},{10,12},{12,14},{1,3},{3,5},{5,7},{... | collective-permute-start | bytes 1572872 | tf_op jit(solution)/shard_map/ppermute | solution.py:26
  772.6 25.0 %collective-permute-start.5 = (bf16[8,128,256]{1,2,0:T(8,128)(2,1)S(1)}, bf16[8,128,256]{1,2,0:T(8,128)(2,1)S(1)}, u32[]{:S(2)}, u32[]{:S(2)}) collective-permute-start(bf16[8,128,256]{1,2,0:T(8,128)(2,1)S(1)} %get-tuple-element.224), channel_id=1, source_target_pairs={{2,0},{4,2},{6,4},{8,6},{10,8},{12,10},{14,12},{3,1},{5,3},{7,5},{... | collective-permute-start | bytes 1572872 | tf_op jit(solution)/shard_map/ppermute | solution.py:26
  797.9 2.6 copy-start.14
  797.9 3.0 copy-start.15
  803.2 46.9 %all-reduce.8.cloned.1.call-start = ((), (), s32[]{:S(2)}) async-start(), calls=%async_computation | async-start | bytes 1310720 | tf_op jit(solution)/shard_map/psum | solution.py:194
  806.4 114.2 %all-reduce.10.cloned.1.call-start = ((), (), s32[]{:S(2)}) async-start(), calls=%async_computation.1 | async-start | bytes 655360 | tf_op jit(solution)/shard_map/psum | solution.py:183
  835.3 9.7 %copy-start.18 = (bf16[128,512]{1,0:T(8,128)(2,1)S(1)}, bf16[128,512]{1,0:T(8,128)(2,1)}, u32[]{:S(2)}) copy-start(bf16[128,512]{1,0:T(8,128)(2,1)} %copy-done.17) | copy-start | bytes 393220
  (35 other events, 59.9 us)
Sparse Core Ops, SparseCore 0:
  803.3 18.8 all-reduce.11
  824.7 20.1 all-reduce.7
  848.9 71.6 all-reduce.9
